TPU v7x, 32 devices: a whole 2x2x4 slice. The times are simulated.
32 devices in a mesh: fsdp: 16 (over z, x, core), dp: 2 (over y).
Axes of the slice: x: 2, y: 2, z: 4, core: 2. Of those that a mesh axis runs over, the one named last changes fastest.
Arguments:
- tokens: bfloat16 [24576, 1024], P(('fsdp', 'dp')), may hold values from -6 to 6
- cotangent: bfloat16 [24576, 1024], P(('fsdp', 'dp')), may hold values from -6 to 6
- segments: int32 [24576], replicated, may hold values from 0 to 47, never falling along the last dimension, each value on 1 to 577 neighbouring positions
- adapter_ids: int32 [48], replicated, may hold values from 0 to 7
- ln1_gain: float32 [1024], replicated, may hold values from 0.5 to 1.5
- ln1_bias: float32 [1024], replicated, may hold values from -1.5 to 1.5
- w_query: bfloat16 [1024, 1024], P(('fsdp', 'dp')), may hold values from -0.1875 to 0.1875
- b_query: float32 [1024], replicated, may hold values from -2.5 to 2.5
- w_key: bfloat16 [1024, 1024], P(('fsdp', 'dp')), may hold values from -0.1875 to 0.1875
- w_value: bfloat16 [1024, 1024], P(('fsdp', 'dp')), may hold values from -0.1875 to 0.1875
- b_value: float32 [1024], replicated, may hold values from -2.5 to 2.5
- w_out: bfloat16 [1024, 1024], P(('fsdp', 'dp')), may hold values from -4 to 4
- b_out: float32 [1024], replicated, may hold values from -2.5 to 2.5
- ln2_gain: float32 [1024], replicated, may hold values from 0.5 to 1.5
- ln2_bias: float32 [1024], replicated, may hold values from -1.5 to 1.5
- w_up: bfloat16 [1024, 4096], P(('fsdp', 'dp')), may hold values from -0.1875 to 0.1875
- b_up: float32 [4096], replicated, may hold values from -2.5 to 2.5
- w_down: bfloat16 [4096, 1024], P(('fsdp', 'dp')), may hold values from -0.1875 to 0.1875
- b_down: float32 [1024], replicated, may hold values from -2.5 to 2.5
- query_in: bfloat16 [1024, 128], P(('fsdp', 'dp')), may hold values from -0.1875 to 0.1875
- query_out: bfloat16 [1024, 128], P(('fsdp', 'dp')), may hold values from -0.75 to 0.75
- value_in: bfloat16 [1024, 128], P(('fsdp', 'dp')), may hold values from -0.1875 to 0.1875
- value_out: bfloat16 [1024, 128], P(('fsdp', 'dp')), may hold values from -0.75 to 0.75
- up_in: bfloat16 [1024, 128], P(('fsdp', 'dp')), may hold values from -0.1875 to 0.1875
- up_out: bfloat16 [4096, 128], P(('fsdp', 'dp')), may hold values from -0.75 to 0.75
- down_in: bfloat16 [4096, 128], P(('fsdp', 'dp')), may hold values from -0.1875 to 0.1875
- down_out: bfloat16 [1024, 128], P(('fsdp', 'dp')), may hold values from -0.75 to 0.75
Outputs:
- block_out: bfloat16 [24576, 1024], P(('fsdp', 'dp'))
- grad_input: bfloat16 [24576, 1024], P(('fsdp', 'dp'))
- grad_query_in: float32 [1024, 128], P(('fsdp', 'dp'))
- grad_query_out: float32 [1024, 128], P(('fsdp', 'dp'))
- grad_value_in: float32 [1024, 128], P(('fsdp', 'dp'))
- grad_value_out: float32 [1024, 128], P(('fsdp', 'dp'))
- grad_up_in: float32 [1024, 128], P(('fsdp', 'dp'))
- grad_up_out: float32 [4096, 128], P(('fsdp', 'dp'))
- grad_down_in: float32 [4096, 128], P(('fsdp', 'dp'))
- grad_down_out: float32 [1024, 128], P(('fsdp', 'dp'))
Inputs may be any that keep to these rules, and one draw needn't show every extreme that they name: `segments`: image numbers never fall along the packed order; each image holds 1 to 577 consecutive tokens, and one holds exactly 577.
All inputs are finite; a program needn't handle non-finite values.
Results may differ from a plain program's by a relative error of at most 0.014.
Values may be sent and summed in bfloat16 or wider, within the bound.
No kernel may reach another device: no remote copies, remote signals or barrier semaphores. Data moves between devices by JAX's collectives and lax.ppermute only.
A program may use at most 384 MiB of HBM per device.

v0:
```python
import jax
import jax.numpy as jnp
from jax import lax
from jax.sharding import PartitionSpec as P

HEADS = 16
HALO = 576
RANK = 16
ADAPTERS = 8
epsilon = 1e-05
gelu_slope = 1.702


def extended(array, sides, width):
    for axis, dim in sides:
        devices, length = (lax.axis_size(axis), array.shape[dim])
        up = [(i, (i + 1) % devices) for i in range(devices - 1)]
        down = [(j, i) for i, j in up]
        last = lax.slice_in_dim(array, length - width, length, axis=dim)
        first = lax.slice_in_dim(array, 0, width, axis=dim)
        before = lax.ppermute(last, axis, up)
        after = lax.ppermute(first, axis, down)
        array = jnp.concatenate([before, array, after], axis=dim)
    return array


def from_behind(value, axis, steps):
    count = lax.axis_size(axis)
    first, last = (max(0, -steps), min(count, count - steps))
    return lax.ppermute(value, axis, [(source, source + steps) for source in range(first, last)])


def product(left, right):
    return jnp.dot(left, right, preferred_element_type=jnp.float32)


def times_transposed(left, right):
    return lax.dot_general(
        left, right, (((1,), (1,)), ((), ())), preferred_element_type=jnp.float32
    )


def transposed_times(left, right):
    return lax.dot_general(
        left, right, (((0,), (0,)), ((), ())), preferred_element_type=jnp.float32
    )


def norm_forward(values, gain, shift):
    mean = jnp.mean(values, axis=1, keepdims=True)
    centered = values - mean
    inverse = lax.rsqrt(jnp.mean(centered * centered, axis=1, keepdims=True) + epsilon)
    normed = centered * inverse
    return (normed * gain + shift, normed, inverse)


def norm_backward(grad, normed, inverse, gain):
    scaled = grad * gain
    return inverse * (
        scaled
        - jnp.mean(scaled, axis=1, keepdims=True)
        - normed * jnp.mean(scaled * normed, axis=1, keepdims=True)
    )


def split_heads(block, head_dim):
    return block.reshape(block.shape[0], block.shape[1] // head_dim, head_dim)


def group_scores(query3, key3, same_image, score_scale):
    raw = jnp.einsum("qhd,khd->hqk", query3, key3, preferred_element_type=jnp.float32) * score_scale
    return jnp.where(same_image[None], raw, -1000000000.0)


def local(
    tokens,
    cotangent,
    segments,
    adapter_ids,
    ln1_gain,
    ln1_bias,
    w_query,
    b_query,
    w_key,
    w_value,
    b_value,
    w_out,
    b_out,
    ln2_gain,
    ln2_bias,
    w_up,
    b_up,
    w_down,
    b_down,
    query_in,
    query_out,
    value_in,
    value_out,
    up_in,
    up_out,
    down_in,
    down_out,
):
    row_count, model_width = tokens.shape
    head_dim = model_width // HEADS
    score_scale = head_dim ** (-0.5)
    group_count = max(1, HEADS // 4)
    group_width = model_width // group_count
    gathered = (
        lax.all_gather(w_query, ("fsdp", "dp"), axis=0, tiled=True),
        lax.all_gather(w_key, ("fsdp", "dp"), axis=0, tiled=True),
        lax.all_gather(w_value, ("fsdp", "dp"), axis=0, tiled=True),
        lax.all_gather(w_out, ("fsdp", "dp"), axis=0, tiled=True),
        lax.all_gather(w_up, ("fsdp", "dp"), axis=0, tiled=True),
        lax.all_gather(w_down, ("fsdp", "dp"), axis=0, tiled=True),
        lax.all_gather(query_in, ("fsdp", "dp"), axis=0, tiled=True),
        lax.all_gather(query_out, ("fsdp", "dp"), axis=0, tiled=True),
        lax.all_gather(value_in, ("fsdp", "dp"), axis=0, tiled=True),
        lax.all_gather(value_out, ("fsdp", "dp"), axis=0, tiled=True),
        lax.all_gather(up_in, ("fsdp", "dp"), axis=0, tiled=True),
        lax.all_gather(up_out, ("fsdp", "dp"), axis=0, tiled=True),
        lax.all_gather(down_in, ("fsdp", "dp"), axis=0, tiled=True),
        lax.all_gather(down_out, ("fsdp", "dp"), axis=0, tiled=True),
    )
    (
        full_wq,
        full_wk,
        full_wv,
        full_wo,
        full_wup,
        full_wdown,
        full_qin,
        full_qout,
        full_vin,
        full_vout,
        full_uin,
        full_uout,
        full_din,
        full_dout,
    ) = gathered
    position = lax.axis_index(("fsdp", "dp"))
    padded_seg = jnp.pad(segments, HALO, constant_values=-1)
    seg_window = lax.dynamic_slice_in_dim(padded_seg, position * row_count, row_count + 2 * HALO, 0)
    seg_own = lax.dynamic_slice_in_dim(segments, position * row_count, row_count, 0)
    same_image = seg_own[:, None] == seg_window[None, :]
    image_hot = (
        seg_own[:, None] == jnp.arange(adapter_ids.shape[0], dtype=jnp.int32)[None, :]
    ).astype(jnp.bfloat16)
    adapter_hot = (adapter_ids[:, None] == jnp.arange(ADAPTERS, dtype=jnp.int32)[None, :]).astype(
        jnp.bfloat16
    )
    select = jnp.repeat(product(image_hot, adapter_hot), RANK, axis=1).astype(jnp.bfloat16)
    tokens_f = tokens.astype(jnp.float32)
    normal1, hat_one, inv_one = norm_forward(tokens_f, ln1_gain, ln1_bias)
    normed1 = normal1.astype(jnp.bfloat16)
    low_q = product(normed1, full_qin).astype(jnp.bfloat16) * select
    low_v = product(normed1, full_vin).astype(jnp.bfloat16) * select
    query = (product(normed1, full_wq) + b_query + times_transposed(low_q, full_qout)).astype(
        jnp.bfloat16
    )
    keys = product(normed1, full_wk).astype(jnp.bfloat16)
    values = (product(normed1, full_wv) + b_value + times_transposed(low_v, full_vout)).astype(
        jnp.bfloat16
    )
    window = extended(jnp.concatenate([keys, values], axis=1), ((("fsdp", "dp"), 0),), HALO)
    key_window = window[:, :model_width]
    value_window = window[:, model_width:]
    mixed_parts = []
    log_totals = []
    for head_group in range(group_count):
        first = head_group * group_width
        query3 = split_heads(query[:, first : first + group_width], head_dim)
        key3 = split_heads(key_window[:, first : first + group_width], head_dim)
        value3 = split_heads(value_window[:, first : first + group_width], head_dim)
        scores = group_scores(query3, key3, same_image, score_scale)
        row_max = jnp.max(scores, axis=2, keepdims=True)
        exp_scores = jnp.exp(scores - row_max)
        row_total = jnp.sum(exp_scores, axis=2, keepdims=True)
        softmax_w = (exp_scores / row_total).astype(jnp.bfloat16)
        log_totals.append(row_max + jnp.log(row_total))
        attended = jnp.einsum("hqk,khd->qhd", softmax_w, value3, preferred_element_type=jnp.float32)
        mixed_parts.append(attended.reshape(row_count, group_width))
    mixed = jnp.concatenate(mixed_parts, axis=1).astype(jnp.bfloat16)
    resid = tokens_f + product(mixed, full_wo) + b_out
    normal2, hat_two, inv_two = norm_forward(resid, ln2_gain, ln2_bias)
    normed2 = normal2.astype(jnp.bfloat16)
    low_u = product(normed2, full_uin).astype(jnp.bfloat16) * select
    pre_act = product(normed2, full_wup) + b_up + times_transposed(low_u, full_uout)
    gate_value = 1.0 / (1.0 + jnp.exp(-gelu_slope * pre_act))
    act = (pre_act * gate_value).astype(jnp.bfloat16)
    low_d = product(act, full_din).astype(jnp.bfloat16) * select
    result = resid + product(act, full_wdown) + b_down + times_transposed(low_d, full_dout)
    block_out = result.astype(jnp.bfloat16)
    again = (
        lax.all_gather(w_query, ("fsdp", "dp"), axis=0, tiled=True),
        lax.all_gather(w_key, ("fsdp", "dp"), axis=0, tiled=True),
        lax.all_gather(w_value, ("fsdp", "dp"), axis=0, tiled=True),
        lax.all_gather(w_out, ("fsdp", "dp"), axis=0, tiled=True),
        lax.all_gather(w_up, ("fsdp", "dp"), axis=0, tiled=True),
        lax.all_gather(w_down, ("fsdp", "dp"), axis=0, tiled=True),
        lax.all_gather(query_in, ("fsdp", "dp"), axis=0, tiled=True),
        lax.all_gather(query_out, ("fsdp", "dp"), axis=0, tiled=True),
        lax.all_gather(value_in, ("fsdp", "dp"), axis=0, tiled=True),
        lax.all_gather(value_out, ("fsdp", "dp"), axis=0, tiled=True),
        lax.all_gather(up_in, ("fsdp", "dp"), axis=0, tiled=True),
        lax.all_gather(up_out, ("fsdp", "dp"), axis=0, tiled=True),
        lax.all_gather(down_in, ("fsdp", "dp"), axis=0, tiled=True),
        lax.all_gather(down_out, ("fsdp", "dp"), axis=0, tiled=True),
    )
    (
        back_wq,
        back_wk,
        back_wv,
        back_wo,
        back_wup,
        back_wdown,
        back_qin,
        back_qout,
        back_vin,
        back_vout,
        back_uin,
        back_uout,
        back_din,
        back_dout,
    ) = again
    grad_down_out = transposed_times(cotangent, low_d)
    d_low_d = product(cotangent, back_dout).astype(jnp.bfloat16) * select
    grad_down_in = transposed_times(act, d_low_d)
    d_act = times_transposed(cotangent, back_wdown) + times_transposed(d_low_d, back_din)
    d_pre = (d_act * (gate_value + gelu_slope * pre_act * gate_value * (1.0 - gate_value))).astype(
        jnp.bfloat16
    )
    grad_up_out = transposed_times(d_pre, low_u)
    d_low_u = product(d_pre, back_uout).astype(jnp.bfloat16) * select
    grad_up_in = transposed_times(normed2, d_low_u)
    d_normed2 = times_transposed(d_pre, back_wup) + times_transposed(d_low_u, back_uin)
    d_resid = cotangent.astype(jnp.float32) + norm_backward(d_normed2, hat_two, inv_two, ln2_gain)
    d_attn = d_resid.astype(jnp.bfloat16)
    d_mixed = times_transposed(d_attn, back_wo).astype(jnp.bfloat16)
    query_grads = []
    key_grads = []
    value_grads = []
    for head_group in range(group_count):
        first = head_group * group_width
        query3 = split_heads(query[:, first : first + group_width], head_dim)
        key3 = split_heads(key_window[:, first : first + group_width], head_dim)
        value3 = split_heads(value_window[:, first : first + group_width], head_dim)
        d_out3 = split_heads(d_mixed[:, first : first + group_width], head_dim)
        scores = group_scores(query3, key3, same_image, score_scale)
        exact_probs = jnp.exp(scores - log_totals[head_group])
        softmax_w = exact_probs.astype(jnp.bfloat16)
        d_probs = jnp.einsum("qhd,khd->hqk", d_out3, value3, preferred_element_type=jnp.float32)
        row_delta = jnp.sum(exact_probs * d_probs, axis=2, keepdims=True)
        d_scores = (exact_probs * (d_probs - row_delta)).astype(jnp.bfloat16)
        grad_q3 = (
            jnp.einsum("hqk,khd->qhd", d_scores, key3, preferred_element_type=jnp.float32)
            * score_scale
        )
        grad_k3 = (
            jnp.einsum("hqk,qhd->khd", d_scores, query3, preferred_element_type=jnp.float32)
            * score_scale
        )
        grad_v3 = jnp.einsum("hqk,qhd->khd", softmax_w, d_out3, preferred_element_type=jnp.float32)
        query_grads.append(grad_q3.reshape(row_count, group_width))
        key_grads.append(grad_k3.reshape(grad_k3.shape[0], group_width))
        value_grads.append(grad_v3.reshape(grad_v3.shape[0], group_width))
    d_query = jnp.concatenate(query_grads, axis=1).astype(jnp.bfloat16)
    d_kv_window = jnp.concatenate(key_grads + value_grads, axis=1)
    from_right = from_behind(d_kv_window[:HALO].astype(jnp.bfloat16), ("fsdp", "dp"), -1).astype(
        jnp.float32
    )
    from_left = from_behind(
        d_kv_window[row_count + HALO :].astype(jnp.bfloat16), ("fsdp", "dp"), 1
    ).astype(jnp.float32)
    d_kv_own = d_kv_window[HALO : HALO + row_count]
    d_kv_own = (
        d_kv_own
        + jnp.pad(from_left, ((0, row_count - HALO), (0, 0)))
        + jnp.pad(from_right, ((row_count - HALO, 0), (0, 0)))
    )
    d_keys = d_kv_own[:, :model_width].astype(jnp.bfloat16)
    d_values = d_kv_own[:, model_width:].astype(jnp.bfloat16)
    grad_query_out = transposed_times(d_query, low_q)
    grad_value_out = transposed_times(d_values, low_v)
    d_low_q = product(d_query, back_qout).astype(jnp.bfloat16) * select
    d_low_v = product(d_values, back_vout).astype(jnp.bfloat16) * select
    grad_query_in = transposed_times(normed1, d_low_q)
    grad_value_in = transposed_times(normed1, d_low_v)
    d_normed1 = (
        times_transposed(d_query, back_wq)
        + times_transposed(d_keys, back_wk)
        + times_transposed(d_values, back_wv)
    )
    d_normed1 = (
        d_normed1 + times_transposed(d_low_q, back_qin) + times_transposed(d_low_v, back_vin)
    )
    grad_input = (d_resid + norm_backward(d_normed1, hat_one, inv_one, ln1_gain)).astype(
        jnp.bfloat16
    )
    summed = (
        lax.psum_scatter(grad_query_in, ("fsdp", "dp"), scatter_dimension=0, tiled=True),
        lax.psum_scatter(grad_query_out, ("fsdp", "dp"), scatter_dimension=0, tiled=True),
        lax.psum_scatter(grad_value_in, ("fsdp", "dp"), scatter_dimension=0, tiled=True),
        lax.psum_scatter(grad_value_out, ("fsdp", "dp"), scatter_dimension=0, tiled=True),
        lax.psum_scatter(grad_up_in, ("fsdp", "dp"), scatter_dimension=0, tiled=True),
        lax.psum_scatter(grad_up_out, ("fsdp", "dp"), scatter_dimension=0, tiled=True),
        lax.psum_scatter(grad_down_in, ("fsdp", "dp"), scatter_dimension=0, tiled=True),
        lax.psum_scatter(grad_down_out, ("fsdp", "dp"), scatter_dimension=0, tiled=True),
    )
    return (
        block_out,
        grad_input,
        summed[0],
        summed[1],
        summed[2],
        summed[3],
        summed[4],
        summed[5],
        summed[6],
        summed[7],
    )


def solution(mesh):
    return jax.shard_map(
        local,
        mesh=mesh,
        in_specs=(
            P(("fsdp", "dp"), None),
            P(("fsdp", "dp"), None),
            P(),
            P(),
            P(),
            P(),
            P(("fsdp", "dp"), None),
            P(),
            P(("fsdp", "dp"), None),
            P(("fsdp", "dp"), None),
            P(),
            P(("fsdp", "dp"), None),
            P(),
            P(),
            P(),
            P(("fsdp", "dp"), None),
            P(),
            P(("fsdp", "dp"), None),
            P(),
            P(("fsdp", "dp"), None),
            P(("fsdp", "dp"), None),
            P(("fsdp", "dp"), None),
            P(("fsdp", "dp"), None),
            P(("fsdp", "dp"), None),
            P(("fsdp", "dp"), None),
            P(("fsdp", "dp"), None),
            P(("fsdp", "dp"), None),
        ),
        out_specs=(
            P(("fsdp", "dp"), None),
            P(("fsdp", "dp"), None),
            P(("fsdp", "dp"), None),
            P(("fsdp", "dp"), None),
            P(("fsdp", "dp"), None),
            P(("fsdp", "dp"), None),
            P(("fsdp", "dp"), None),
            P(("fsdp", "dp"), None),
            P(("fsdp", "dp"), None),
            P(("fsdp", "dp"), None),
        ),
        check_vma=False,
    )
```

profile of v0, /device:TPU:0, one launch (start us, length us, event | category | flops | bytes accessed | tf_op | source)
XLA Modules:
  0.0 2053.9 jit_solution(11524287528089910341)
XLA Ops:
  16.4 76.2 %all_gather.61 = bf16[1024,128]{1,0:T(8,128)(2,1)} all-gather(bf16[32,128]{1,0:T(8,128)(2,1)S(1)} %copy-done.96), channel_id=1, replica_groups=mesh['fsdp'=16,'dp'=2] {'fsdp','dp'}, dimensions={0}, use_global_device_ids=true | all-gather | bytes 270336 | tf_op jit(solution)/shard_map/all_gather | solution.py:116
  92.6 70.0 %all_gather.62 = bf16[1024,128]{1,0:T(8,128)(2,1)} all-gather(bf16[32,128]{1,0:T(8,128)(2,1)S(1)} %copy-done.97), channel_id=1, replica_groups=mesh['fsdp'=16,'dp'=2] {'fsdp','dp'}, dimensions={0}, use_global_device_ids=true | all-gather | bytes 270336 | tf_op jit(solution)/shard_map/all_gather | solution.py:117
  162.6 67.6 %all_gather.58 = bf16[1024,128]{1,0:T(8,128)(2,1)S(1)} all-gather(bf16[32,128]{1,0:T(8,128)(2,1)S(1)} %copy-done.98), channel_id=1, replica_groups=mesh['fsdp'=16,'dp'=2] {'fsdp','dp'}, dimensions={0}, use_global_device_ids=true | all-gather | bytes 270336 | tf_op jit(solution)/shard_map/all_gather | solution.py:118
  230.2 70.7 %all_gather.59 = bf16[1024,128]{1,0:T(8,128)(2,1)} all-gather(bf16[32,128]{1,0:T(8,128)(2,1)S(1)} %copy-done.99), channel_id=1, replica_groups=mesh['fsdp'=16,'dp'=2] {'fsdp','dp'}, dimensions={0}, use_global_device_ids=true | all-gather | bytes 270336 | tf_op jit(solution)/shard_map/all_gather | solution.py:119
  300.9 73.3 %all_gather.65 = bf16[1024,128]{1,0:T(8,128)(2,1)} all-gather(bf16[32,128]{1,0:T(8,128)(2,1)S(1)} %copy-done.100), channel_id=1, replica_groups=mesh['fsdp'=16,'dp'=2] {'fsdp','dp'}, dimensions={0}, use_global_device_ids=true | all-gather | bytes 270336 | tf_op jit(solution)/shard_map/all_gather | solution.py:120
  394.6 160.8 %all_gather.69 = bf16[1024,128]{1,0:T(8,128)(2,1)S(1)} all-gather(bf16[32,128]{1,0:T(8,128)(2,1)S(1)} %copy-done.101), channel_id=1, replica_groups=mesh['fsdp'=16,'dp'=2] {'fsdp','dp'}, dimensions={0}, use_global_device_ids=true | all-gather | bytes 270336 | tf_op jit(solution)/shard_map/all_gather | solution.py:123
  732.0 12.3 fusion.97
  756.5 13.5 multiply_convert_fusion.5
  813.0 18.6 multiply_reduce_fusion
  831.5 15.7 multiply_convert_fusion
  865.0 18.8 multiply_reduce_fusion.1
  895.1 18.6 multiply_reduce_fusion.2
  925.1 18.6 multiply_reduce_fusion.3
  957.4 15.7 multiply_convert_fusion.1
  979.3 15.7 multiply_convert_fusion.2
  1001.1 15.8 multiply_convert_fusion.3
  1093.9 48.1 %collective-permute-done.2 = bf16[576,2048]{1,0:T(8,128)(2,1)} collective-permute-done((bf16[576,2048]{1,0:T(8,128)(2,1)}, bf16[576,2048]{1,0:T(8,128)(2,1)}, u32[]{:S(2)}, u32[]{:S(2)}) %collective-permute-start.2) | collective-permute-done | bytes 2359328 | tf_op jit(solution)/shard_map/ppermute | solution.py:30
  1193.1 41.3 %reduce-scatter.25.cloned.1.call-done = f32[32,128]{1,0:T(8,128)} async-done(((f32[1024,128]{1,0:T(8,128)}), f32[32,128]{1,0:T(8,128)}) %reduce-scatter.25.cloned.1.call-update) | async-done | bytes 16400
  1234.4 134.7 %reduce-scatter.13.cloned.1.call-done = f32[32,128]{1,0:T(8,128)} async-done(((f32[1024,128]{1,0:T(8,128)}), f32[32,128]{1,0:T(8,128)}) %reduce-scatter.13.cloned.1.call-update) | async-done | bytes 16400 | tf_op jit(solution)/shard_map/reduce_scatter | solution.py:302
  1369.1 134.3 %reduce-scatter.11.cloned.1.call-done = f32[32,128]{1,0:T(8,128)} async-done(((f32[1024,128]{1,0:T(8,128)}), f32[32,128]{1,0:T(8,128)}) %reduce-scatter.11.cloned.1.call-update) | async-done | bytes 16400 | tf_op jit(solution)/shard_map/reduce_scatter | solution.py:301
  1503.4 134.5 %reduce-scatter.15.cloned.1.call-done = f32[32,128]{1,0:T(8,128)} async-done(((f32[1024,128]{1,0:T(8,128)}), f32[32,128]{1,0:T(8,128)}) %reduce-scatter.15.cloned.1.call-update) | async-done | bytes 16400 | tf_op jit(solution)/shard_map/reduce_scatter | solution.py:303
  1637.9 134.3 %reduce-scatter.17.cloned.1.call-done = f32[32,128]{1,0:T(8,128)} async-done(((f32[1024,128]{1,0:T(8,128)}), f32[32,128]{1,0:T(8,128)}) %reduce-scatter.17.cloned.1.call-update) | async-done | bytes 16400 | tf_op jit(solution)/shard_map/reduce_scatter | solution.py:304
  1772.2 137.1 %reduce-scatter.21.cloned.1.call-done = f32[128,128]{1,0:T(8,128)} async-done(((f32[4096,128]{1,0:T(8,128)}), f32[128,128]{1,0:T(8,128)}) %reduce-scatter.21.cloned.1.call-update) | async-done | bytes 65552 | tf_op jit(solution)/shard_map/reduce_scatter | solution.py:306
  1909.3 137.8 %reduce-scatter.23.cloned.1.call-done = f32[128,128]{1,0:T(8,128)} async-done(((f32[4096,128]{1,0:T(8,128)}), f32[128,128]{1,0:T(8,128)}) %reduce-scatter.23.cloned.1.call-update) | async-done | bytes 65552 | tf_op jit(solution)/shard_map/reduce_scatter | solution.py:307
  (399 shorter events, 454.2 us)
Async XLA Ops:
  7.2 367.0 %copy-start.94 = (f32[1024]{0:T(1024)S(1)}, f32[1024]{0:T(1024)}, u32[]{:S(2)}) copy-start(f32[1024]{0:T(1024)} %param.31) | copy-start | bytes 12292
  7.3 366.9 %copy-start.102 = (f32[1024]{0:T(1024)S(1)}, f32[1024]{0:T(1024)}, u32[]{:S(2)}) copy-start(f32[1024]{0:T(1024)} %param.32) | copy-start | bytes 12292
  7.3 368.2 %all-gather.11.cloned.1.call-start = ((), (), s32[]{:S(2)}) async-start(), calls=%async_computation.9 | async-start | bytes 2162688 | tf_op jit(solution)/shard_map/all_gather | solution.py:112
  8.0 372.3 %all-gather.9.cloned.1.call-start = ((), (), s32[]{:S(2)}) async-start(), calls=%async_computation.8 | async-start | bytes 2162688 | tf_op jit(solution)/shard_map/all_gather | solution.py:111
  8.8 550.1 %all-gather.13.cloned.1.call-start = ((), (), s32[]{:S(2)}) async-start(), calls=%async_computation.10 | async-start | bytes 2162688 | tf_op jit(solution)/shard_map/all_gather | solution.py:110
  9.5 714.4 %all-gather.15.cloned.1.call-start = ((), (), s32[]{:S(2)}) async-start(), calls=%async_computation.11 | async-start | bytes 2162688 | tf_op jit(solution)/shard_map/all_gather | solution.py:113
  10.1 722.0 %all-gather.21.cloned.1.call-start = ((), (), s32[]{:S(2)}) async-start(), calls=%async_computation.14 | async-start | bytes 8650752 | tf_op jit(solution)/shard_map/all_gather | solution.py:115
  10.7 733.7 %all-gather.17.cloned.1.call-start = ((), (), s32[]{:S(2)}) async-start(), calls=%async_computation.12 | async-start | bytes 8650752 | tf_op jit(solution)/shard_map/all_gather | solution.py:114
  11.2 745.2 %all-gather.19.cloned.1.call-start = ((), (), s32[]{:S(2)}) async-start(), calls=%async_computation.13 | async-start | bytes 1081344 | tf_op jit(solution)/shard_map/all_gather | solution.py:121
  12.0 758.0 %all-gather.23.cloned.1.call-start = ((), (), s32[]{:S(2)}) async-start(), calls=%async_computation.15 | async-start | bytes 1081344 | tf_op jit(solution)/shard_map/all_gather | solution.py:122
  12.7 1180.4 %reduce-scatter.19.cloned.1.call-start = ((), (), s32[]{:S(2)}) async-start(), calls=%async_computation.20 | async-start | bytes 540672 | tf_op jit(solution)/shard_map/reduce_scatter | solution.py:305
  14.5 359.7 %copy-start.89 = (f32[768]{0:T(1024)}, f32[768]{0:T(1024)S(1)}, u32[]{:S(2)}) copy-start(f32[768]{0:T(1024)S(1)} %broadcast_multiply_fusion.5) | copy-start | bytes 9220
  16.4 540.3 %copy-start.45 = (bf16[768,128]{1,0:T(8,128)(2,1)}, bf16[768,128]{1,0:T(8,128)(2,1)S(1)}, u32[]{:S(2)}) copy-start(bf16[768,128]{1,0:T(8,128)(2,1)S(1)} %copy.96) | copy-start | bytes 589828
  390.5 180.3 %collective-permute-start = (bf16[576,2048]{1,0:T(8,128)(2,1)}, bf16[576,2048]{1,0:T(8,128)(2,1)}, u32[]{:S(2)}, u32[]{:S(2)}) collective-permute-start(bf16[576,2048]{1,0:T(8,128)(2,1)} %get-tuple-element.54), channel_id=1, source_target_pairs={{0,1},{1,2},{2,3},{3,4},{4,5},{5,6},{6,7},{7,8},{8,9},{9,10},{10,1... | collective-permute-start | bytes 7077896 | tf_op jit(solution)/shard_map/ppermute | solution.py:21
  393.2 177.6 %collective-permute-start.1 = (bf16[576,2048]{1,0:T(8,128)(2,1)}, bf16[576,2048]{1,0:T(8,128)(2,1)}, u32[]{:S(2)}, u32[]{:S(2)}) collective-permute-start(bf16[576,2048]{1,0:T(8,128)(2,1)} %get-tuple-element.55), channel_id=1, source_target_pairs={{1,0},{2,1},{3,2},{4,3},{5,4},{6,5},{7,6},{8,7},{9,8},{10,9},{11,1... | collective-permute-start | bytes 7077896 | tf_op jit(solution)/shard_map/ppermute | solution.py:22
  943.7 290.6 %reduce-scatter.25.cloned.1.call-start = ((), (), s32[]{:S(2)}) async-start(), calls=%async_computation.23 | async-start | bytes 540672
  1058.4 83.6 %collective-permute-start.2 = (bf16[576,2048]{1,0:T(8,128)(2,1)}, bf16[576,2048]{1,0:T(8,128)(2,1)}, u32[]{:S(2)}, u32[]{:S(2)}) collective-permute-start(bf16[576,2048]{1,0:T(8,128)(2,1)} %get-tuple-element.44), channel_id=1, source_target_pairs={{0,1},{1,2},{2,3},{3,4},{4,5},{5,6},{6,7},{7,8},{8,9},{9,10},{10,1... | collective-permute-start | bytes 7077896 | tf_op jit(solution)/shard_map/ppermute | solution.py:30
  1062.7 80.0 %collective-permute-start.3 = (bf16[576,2048]{1,0:T(8,128)(2,1)}, bf16[576,2048]{1,0:T(8,128)(2,1)}, u32[]{:S(2)}, u32[]{:S(2)}) collective-permute-start(bf16[576,2048]{1,0:T(8,128)(2,1)} %get-tuple-element.45), channel_id=1, source_target_pairs={{1,0},{2,1},{3,2},{4,3},{5,4},{6,5},{7,6},{8,7},{9,8},{10,9},{11,1... | collective-permute-start | bytes 7077896 | tf_op jit(solution)/shard_map/ppermute | solution.py:30
  1072.2 296.9 %reduce-scatter.13.cloned.1.call-start = ((), (), s32[]{:S(2)}) async-start(), calls=%async_computation.17 | async-start | bytes 540672 | tf_op jit(solution)/shard_map/reduce_scatter | solution.py:302
  1089.9 413.5 %reduce-scatter.11.cloned.1.call-start = ((), (), s32[]{:S(2)}) async-start(), calls=%async_computation.16 | async-start | bytes 540672 | tf_op jit(solution)/shard_map/reduce_scatter | solution.py:301
  1093.8 544.1 %reduce-scatter.15.cloned.1.call-start = ((), (), s32[]{:S(2)}) async-start(), calls=%async_computation.18 | async-start | bytes 540672 | tf_op jit(solution)/shard_map/reduce_scatter | solution.py:303
  1152.1 620.1 %reduce-scatter.17.cloned.1.call-start = ((), (), s32[]{:S(2)}) async-start(), calls=%async_computation.19 | async-start | bytes 540672 | tf_op jit(solution)/shard_map/reduce_scatter | solution.py:304
  1155.0 754.3 %reduce-scatter.21.cloned.1.call-start = ((), (), s32[]{:S(2)}) async-start(), calls=%async_computation.21 | async-start | bytes 2162688 | tf_op jit(solution)/shard_map/reduce_scatter | solution.py:306
  1161.1 886.1 %reduce-scatter.23.cloned.1.call-start = ((), (), s32[]{:S(2)}) async-start(), calls=%async_computation.22 | async-start | bytes 2162688 | tf_op jit(solution)/shard_map/reduce_scatter | solution.py:307
  (110 other events, 2627.4 us)
Sparse Core Ops, SparseCore 0:
  11.2 59.3 all-gather.10
  73.7 55.3 all-gather.8
  132.2 55.6 all-gather.12
  190.8 55.3 all-gather.14
  249.2 77.4 all-gather.20
  329.6 112.4 all-gather.16
  445.0 55.7 all-gather.18
  503.6 52.7 all-gather.22
  943.9 150.1 reduce-scatter.18
  1096.7 137.6 reduce-scatter.24
  1237.2 131.8 reduce-scatter.12
  1371.8 131.6 reduce-scatter.10
  1506.2 131.6 reduce-scatter.14
  1640.6 131.6 reduce-scatter.16
  1774.9 134.3 reduce-scatter.20
  1912.0 135.1 reduce-scatter.22
where the time goes:
time: 2060 us; the launch traced here: 2050 us
  waiting for transfers between devices  908 us (44%)
  blocking collectives  519 us (25%)
  matrix products  376 us (18%)
  other arithmetic  140 us (7%)
  local copies, waits for them, and re-layouts  84.7 us (4%)
    all_gather x1, blocking collectives, local(): lax.all_gather(down_out, ('fsdp', 'dp'), axis=0, tiled=True)  161 us
    reduce_scatter x1, waiting for transfers between devices, local(): lax.psum_scatter(grad_down_in, ('fsdp', 'dp'), scatter_dimension=0, tiled...  138 us
    reduce_scatter x1, waiting for transfers between devices, local(): lax.psum_scatter(grad_up_out, ('fsdp', 'dp'), scatter_dimension=0, tiled=...  137 us
    reduce_scatter x1, waiting for transfers between devices, local(): lax.psum_scatter(grad_query_out, ('fsdp', 'dp'), scatter_dimension=0, til...  135 us
    reduce_scatter x1, waiting for transfers between devices, local(): lax.psum_scatter(grad_value_in, ('fsdp', 'dp'), scatter_dimension=0, tile...  135 us
    reduce_scatter x1, waiting for transfers between devices, local(): lax.psum_scatter(grad_value_out, ('fsdp', 'dp'), scatter_dimension=0, til...  134 us
    reduce_scatter x1, waiting for transfers between devices, local(): lax.psum_scatter(grad_query_in, ('fsdp', 'dp'), scatter_dimension=0, tile...  134 us
    all_gather x1, blocking collectives, local(): lax.all_gather(query_in, ('fsdp', 'dp'), axis=0, tiled=True)  76.2 us
  transfers between devices with their start and end apart: 20, of which 9 were waited for; matrix products, arithmetic and copies ran while one was open for 20% of the time, Pallas kernels for 0%

commit v1 on v0

--- a/solution.py
+++ b/solution.py
@@ -9,6 +9,28 @@
 ADAPTERS = 8
 epsilon = 1e-05
 gelu_slope = 1.702
+
+
+def laid_out(parts, dim):
+    dims = list(parts.shape[1:])
+    dims[dim] *= parts.shape[0]
+    return jnp.moveaxis(parts, 0, dim).reshape(dims)
+
+
+def grow_blocks(shard, axis):
+    size = lax.axis_size(axis)
+    blocks = shard[None]
+    for level in range(size.bit_length() - 1):
+        distance = 1 << level
+        theirs = lax.ppermute(blocks, axis, [(i, i ^ distance) for i in range(size)])
+        both = jnp.stack([blocks, theirs])
+        upper = lax.axis_index(axis) >> level & 1
+        blocks = jnp.where(upper == 0, both, both[::-1]).reshape(-1, *shard.shape)
+    return blocks
+
+
+def gather_by_bits(x, axis, dim):
+    return laid_out(grow_blocks(x, axis), dim)
 
 
 def extended(array, sides, width):
@@ -116,7 +138,7 @@
         lax.all_gather(query_in, ("fsdp", "dp"), axis=0, tiled=True),
         lax.all_gather(query_out, ("fsdp", "dp"), axis=0, tiled=True),
         lax.all_gather(value_in, ("fsdp", "dp"), axis=0, tiled=True),
-        lax.all_gather(value_out, ("fsdp", "dp"), axis=0, tiled=True),
+        gather_by_bits(value_out, ("fsdp", "dp"), 0),
         lax.all_gather(up_in, ("fsdp", "dp"), axis=0, tiled=True),
         lax.all_gather(up_out, ("fsdp", "dp"), axis=0, tiled=True),
         lax.all_gather(down_in, ("fsdp", "dp"), axis=0, tiled=True),

time: 2060 us -> 2010 us (0.976)
  waiting for transfers between devices: 908 us -> 769 us
  blocking collectives: 519 us -> 602 us
    all_gather x1, blocking collectives: 70.7 us -> 143 us  [local(): lax.all_gather(value_out, ('fsdp', 'dp'), axis=0, tiled=True)]
    reduce_scatter x1, waiting for transfers between devices: 135 us -> 84.1 us  [local(): lax.psum_scatter(grad_query_out, ('fsdp', 'dp'), scatter_dimension=0, til...]
    ppermute x2, waiting for transfers between devices: 48.8 us -> 0.01 us  [from_behind(): lax.ppermute(value, axis, [(source, source + steps) for source in range(f...]
    unnamed x17, waiting for transfers between devices: 46.4 us -> 4.48 us
  transfers between devices with their start and end apart: 20 -> 25, of which waited for: 9 -> 7; matrix products, arithmetic and copies ran while one was open for 20% -> 21% of each run, Pallas kernels for 0% -> 0%
where the time goes in v1:
time: 2010 us; the launch traced here: 2000 us
  waiting for transfers between devices  769 us (38%)
  blocking collectives  602 us (30%)
  matrix products  376 us (19%)
  other arithmetic  141 us (7%)
  local copies, waits for them, and re-layouts  83.4 us (4%)
    all_gather x1, blocking collectives, local(): lax.all_gather(down_out, ('fsdp', 'dp'), axis=0, tiled=True)  177 us
    all_gather x1, blocking collectives, local(): lax.all_gather(value_out, ('fsdp', 'dp'), axis=0, tiled=True)  143 us
    reduce_scatter x1, waiting for transfers between devices, local(): lax.psum_scatter(grad_down_in, ('fsdp', 'dp'), scatter_dimension=0, tiled...  137 us
    reduce_scatter x1, waiting for transfers between devices, local(): lax.psum_scatter(grad_up_out, ('fsdp', 'dp'), scatter_dimension=0, tiled=...  137 us
    reduce_scatter x1, waiting for transfers between devices, local(): lax.psum_scatter(grad_value_in, ('fsdp', 'dp'), scatter_dimension=0, tile...  134 us
    reduce_scatter x1, waiting for transfers between devices, local(): lax.psum_scatter(grad_value_out, ('fsdp', 'dp'), scatter_dimension=0, til...  134 us
    reduce_scatter x1, waiting for transfers between devices, local(): lax.psum_scatter(grad_query_in, ('fsdp', 'dp'), scatter_dimension=0, tile...  134 us
    reduce_scatter x1, waiting for transfers between devices, local(): lax.psum_scatter(grad_query_out, ('fsdp', 'dp'), scatter_dimension=0, til...  84.1 us
  transfers between devices with their start and end apart: 25, of which 7 were waited for; matrix products, arithmetic and copies ran while one was open for 21% of the time, Pallas kernels for 0%

profile of v1, /device:TPU:0, one launch (start us, length us, event | category | flops | bytes accessed | tf_op | source)
XLA Modules:
  0.0 2002.4 jit_solution(12745363326962083792)
XLA Ops:
  19.4 69.7 %all_gather.57 = bf16[1024,128]{1,0:T(8,128)(2,1)S(1)} all-gather(bf16[32,128]{1,0:T(8,128)(2,1)S(1)} %copy-done.94), channel_id=1, replica_groups=mesh['fsdp'=16,'dp'=2] {'fsdp','dp'}, dimensions={0}, use_global_device_ids=true | all-gather | bytes 270336 | tf_op jit(solution)/shard_map/all_gather | solution.py:140
  93.4 70.1 %all_gather.59 = bf16[1024,128]{1,0:T(8,128)(2,1)} all-gather(bf16[32,128]{1,0:T(8,128)(2,1)S(1)} %copy-done.95), channel_id=1, replica_groups=mesh['fsdp'=16,'dp'=2] {'fsdp','dp'}, dimensions={0}, use_global_device_ids=true | all-gather | bytes 270336 | tf_op jit(solution)/shard_map/all_gather | solution.py:138
  163.7 72.1 %all_gather.60 = bf16[1024,128]{1,0:T(8,128)(2,1)} all-gather(bf16[32,128]{1,0:T(8,128)(2,1)S(1)} %copy-done.96), channel_id=1, replica_groups=mesh['fsdp'=16,'dp'=2] {'fsdp','dp'}, dimensions={0}, use_global_device_ids=true | all-gather | bytes 270336 | tf_op jit(solution)/shard_map/all_gather | solution.py:139
  235.8 70.9 %all_gather.63 = bf16[1024,128]{1,0:T(8,128)(2,1)} all-gather(bf16[32,128]{1,0:T(8,128)(2,1)S(1)} %copy-done.97), channel_id=1, replica_groups=mesh['fsdp'=16,'dp'=2] {'fsdp','dp'}, dimensions={0}, use_global_device_ids=true | all-gather | bytes 270336 | tf_op jit(solution)/shard_map/all_gather | solution.py:142
  328.6 176.9 %all_gather.67 = bf16[1024,128]{1,0:T(8,128)(2,1)S(1)} all-gather(bf16[32,128]{1,0:T(8,128)(2,1)S(1)} %copy-done.98), channel_id=1, replica_groups=mesh['fsdp'=16,'dp'=2] {'fsdp','dp'}, dimensions={0}, use_global_device_ids=true | all-gather | bytes 270336 | tf_op jit(solution)/shard_map/all_gather | solution.py:145
  545.0 11.7 fusion.92
  682.1 12.1 fusion.99
  694.3 12.2 fusion.97
  706.4 13.5 multiply_convert_fusion.5
  762.9 18.6 multiply_reduce_fusion
  781.5 15.7 multiply_convert_fusion
  814.9 18.9 multiply_reduce_fusion.1
  845.1 18.6 multiply_reduce_fusion.2
  875.1 18.6 multiply_reduce_fusion.3
  907.5 15.8 multiply_convert_fusion.1
  929.5 15.7 multiply_convert_fusion.2
  951.3 15.7 multiply_convert_fusion.3
  1038.2 142.8 %all_gather.68 = bf16[1024,128]{1,0:T(8,128)(2,1)} all-gather(bf16[32,128]{1,0:T(8,128)(2,1)S(1)} %copy-done.90), channel_id=1, replica_groups=mesh['fsdp'=16,'dp'=2] {'fsdp','dp'}, dimensions={0}, use_global_device_ids=true | all-gather | bytes 270336 | tf_op jit(solution)/shard_map/all_gather | solution.py:226
  1234.1 84.1 %reduce-scatter.13.cloned.1.call-done = f32[32,128]{1,0:T(8,128)} async-done(((f32[1024,128]{1,0:T(8,128)}), f32[32,128]{1,0:T(8,128)}) %reduce-scatter.13.cloned.1.call-update) | async-done | bytes 16400 | tf_op jit(solution)/shard_map/reduce_scatter | solution.py:324
  1318.2 134.3 %reduce-scatter.11.cloned.1.call-done = f32[32,128]{1,0:T(8,128)} async-done(((f32[1024,128]{1,0:T(8,128)}), f32[32,128]{1,0:T(8,128)}) %reduce-scatter.11.cloned.1.call-update) | async-done | bytes 16400 | tf_op jit(solution)/shard_map/reduce_scatter | solution.py:323
  1452.5 134.5 %reduce-scatter.15.cloned.1.call-done = f32[32,128]{1,0:T(8,128)} async-done(((f32[1024,128]{1,0:T(8,128)}), f32[32,128]{1,0:T(8,128)}) %reduce-scatter.15.cloned.1.call-update) | async-done | bytes 16400 | tf_op jit(solution)/shard_map/reduce_scatter | solution.py:325
  1587.0 134.4 %reduce-scatter.17.cloned.1.call-done = f32[32,128]{1,0:T(8,128)} async-done(((f32[1024,128]{1,0:T(8,128)}), f32[32,128]{1,0:T(8,128)}) %reduce-scatter.17.cloned.1.call-update) | async-done | bytes 16400 | tf_op jit(solution)/shard_map/reduce_scatter | solution.py:326
  1721.4 136.7 %reduce-scatter.21.cloned.1.call-done = f32[128,128]{1,0:T(8,128)} async-done(((f32[4096,128]{1,0:T(8,128)}), f32[128,128]{1,0:T(8,128)}) %reduce-scatter.21.cloned.1.call-update) | async-done | bytes 65552 | tf_op jit(solution)/shard_map/reduce_scatter | solution.py:328
  1858.0 137.5 %reduce-scatter.23.cloned.1.call-done = f32[128,128]{1,0:T(8,128)} async-done(((f32[4096,128]{1,0:T(8,128)}), f32[128,128]{1,0:T(8,128)}) %reduce-scatter.23.cloned.1.call-update) | async-done | bytes 65552 | tf_op jit(solution)/shard_map/reduce_scatter | solution.py:329
  (413 shorter events, 435.5 us)
Async XLA Ops:
  7.2 300.2 %all-gather.11.cloned.1.call-start = ((), (), s32[]{:S(2)}) async-start(), calls=%async_computation.9 | async-start | bytes 2162688 | tf_op jit(solution)/shard_map/all_gather | solution.py:134
  7.9 303.6 %all-gather.9.cloned.1.call-start = ((), (), s32[]{:S(2)}) async-start(), calls=%async_computation.8 | async-start | bytes 2162688 | tf_op jit(solution)/shard_map/all_gather | solution.py:133
  8.7 500.3 %all-gather.13.cloned.1.call-start = ((), (), s32[]{:S(2)}) async-start(), calls=%async_computation.10 | async-start | bytes 2162688 | tf_op jit(solution)/shard_map/all_gather | solution.py:132
  9.4 664.5 %all-gather.15.cloned.1.call-start = ((), (), s32[]{:S(2)}) async-start(), calls=%async_computation.11 | async-start | bytes 2162688 | tf_op jit(solution)/shard_map/all_gather | solution.py:135
  10.0 672.1 %all-gather.21.cloned.1.call-start = ((), (), s32[]{:S(2)}) async-start(), calls=%async_computation.14 | async-start | bytes 8650752 | tf_op jit(solution)/shard_map/all_gather | solution.py:137
  10.6 683.7 %all-gather.17.cloned.1.call-start = ((), (), s32[]{:S(2)}) async-start(), calls=%async_computation.12 | async-start | bytes 8650752 | tf_op jit(solution)/shard_map/all_gather | solution.py:136
  11.2 695.3 %all-gather.19.cloned.1.call-start = ((), (), s32[]{:S(2)}) async-start(), calls=%async_computation.13 | async-start | bytes 1081344 | tf_op jit(solution)/shard_map/all_gather | solution.py:143
  11.9 708.0 %all-gather.23.cloned.1.call-start = ((), (), s32[]{:S(2)}) async-start(), calls=%async_computation.15 | async-start | bytes 1081344 | tf_op jit(solution)/shard_map/all_gather | solution.py:144
  12.0 7.3 collective-permute-start
  15.0 1219.0 %reduce-scatter.19.cloned.1.call-start = ((), (), s32[]{:S(2)}) async-start(), calls=%async_computation.20 | async-start | bytes 540672 | tf_op jit(solution)/shard_map/reduce_scatter | solution.py:327
  19.3 70.0 %collective-permute-start.1 = (bf16[2,32,128]{2,1,0:T(8,128)(2,1)S(1)}, bf16[2,32,128]{2,1,0:T(8,128)(2,1)S(1)}, u32[]{:S(2)}, u32[]{:S(2)}) collective-permute-start(bf16[2,32,128]{2,1,0:T(8,128)(2,1)S(1)} %get-tuple-element.65), channel_id=1, source_target_pairs={{0,2},{1,3},{2,0},{3,1},{4,6},{5,7},{6,4},{7,5},{8,10},{9,11},{10,... | collective-permute-start | bytes 49160 | tf_op jit(solution)/shard_map/ppermute | solution.py:25
  93.3 70.2 %collective-permute-start.3 = (bf16[8,32,128]{2,1,0:T(8,128)(2,1)S(1)}, bf16[8,32,128]{2,1,0:T(8,128)(2,1)S(1)}, u32[]{:S(2)}, u32[]{:S(2)}) collective-permute-start(bf16[8,32,128]{2,1,0:T(8,128)(2,1)S(1)} %bitcast.245), channel_id=1, source_target_pairs={{0,8},{1,9},{2,10},{3,11},{4,12},{5,13},{6,14},{7,15},{8,0},{9,1},... | collective-permute-start | bytes 196616 | tf_op jit(solution)/shard_map/ppermute | solution.py:25
  163.6 143.0 %collective-permute-start.4 = (bf16[16,32,128]{2,1,0:T(8,128)(2,1)S(1)}, bf16[16,32,128]{2,1,0:T(8,128)(2,1)S(1)}, u32[]{:S(2)}, u32[]{:S(2)}) collective-permute-start(bf16[16,32,128]{2,1,0:T(8,128)(2,1)S(1)} %bitcast.243), channel_id=1, source_target_pairs={{0,16},{1,17},{2,18},{3,19},{4,20},{5,21},{6,22},{7,23},{8,24},{9,... | collective-permute-start | bytes 393224 | tf_op jit(solution)/shard_map/ppermute | solution.py:25
  321.8 199.0 %collective-permute-start.5 = (bf16[576,2048]{1,0:T(8,128)(2,1)}, bf16[576,2048]{1,0:T(8,128)(2,1)}, u32[]{:S(2)}, u32[]{:S(2)}) collective-permute-start(bf16[576,2048]{1,0:T(8,128)(2,1)} %get-tuple-element.54), channel_id=1, source_target_pairs={{0,1},{1,2},{2,3},{3,4},{4,5},{5,6},{6,7},{7,8},{8,9},{9,10},{10,1... | collective-permute-start | bytes 7077896 | tf_op jit(solution)/shard_map/ppermute | solution.py:43
  327.2 193.6 %collective-permute-start.6 = (bf16[576,2048]{1,0:T(8,128)(2,1)}, bf16[576,2048]{1,0:T(8,128)(2,1)}, u32[]{:S(2)}, u32[]{:S(2)}) collective-permute-start(bf16[576,2048]{1,0:T(8,128)(2,1)} %get-tuple-element.55), channel_id=1, source_target_pairs={{1,0},{2,1},{3,2},{4,3},{5,4},{6,5},{7,6},{8,7},{9,8},{10,9},{11,1... | collective-permute-start | bytes 7077896 | tf_op jit(solution)/shard_map/ppermute | solution.py:44
  893.7 340.4 %reduce-scatter.25.cloned.1.call-start = ((), (), s32[]{:S(2)}) async-start(), calls=%async_computation.23 | async-start | bytes 540672
  1008.2 176.1 %collective-permute-start.7 = (bf16[576,2048]{1,0:T(8,128)(2,1)}, bf16[576,2048]{1,0:T(8,128)(2,1)}, u32[]{:S(2)}, u32[]{:S(2)}) collective-permute-start(bf16[576,2048]{1,0:T(8,128)(2,1)} %get-tuple-element.44), channel_id=1, source_target_pairs={{0,1},{1,2},{2,3},{3,4},{4,5},{5,6},{6,7},{7,8},{8,9},{9,10},{10,1... | collective-permute-start | bytes 7077896 | tf_op jit(solution)/shard_map/ppermute | solution.py:52
  1010.9 173.4 %collective-permute-start.8 = (bf16[576,2048]{1,0:T(8,128)(2,1)}, bf16[576,2048]{1,0:T(8,128)(2,1)}, u32[]{:S(2)}, u32[]{:S(2)}) collective-permute-start(bf16[576,2048]{1,0:T(8,128)(2,1)} %get-tuple-element.45), channel_id=1, source_target_pairs={{1,0},{2,1},{3,2},{4,3},{5,4},{6,5},{7,6},{8,7},{9,8},{10,9},{11,1... | collective-permute-start | bytes 7077896 | tf_op jit(solution)/shard_map/ppermute | solution.py:52
  1020.4 297.8 %reduce-scatter.13.cloned.1.call-start = ((), (), s32[]{:S(2)}) async-start(), calls=%async_computation.17 | async-start | bytes 540672 | tf_op jit(solution)/shard_map/reduce_scatter | solution.py:324
  1038.1 414.4 %reduce-scatter.11.cloned.1.call-start = ((), (), s32[]{:S(2)}) async-start(), calls=%async_computation.16 | async-start | bytes 540672 | tf_op jit(solution)/shard_map/reduce_scatter | solution.py:323
  1184.2 402.8 %reduce-scatter.15.cloned.1.call-start = ((), (), s32[]{:S(2)}) async-start(), calls=%async_computation.18 | async-start | bytes 540672 | tf_op jit(solution)/shard_map/reduce_scatter | solution.py:325
  1192.8 528.5 %reduce-scatter.17.cloned.1.call-start = ((), (), s32[]{:S(2)}) async-start(), calls=%async_computation.19 | async-start | bytes 540672 | tf_op jit(solution)/shard_map/reduce_scatter | solution.py:326
  1195.8 662.2 %reduce-scatter.21.cloned.1.call-start = ((), (), s32[]{:S(2)}) async-start(), calls=%async_computation.21 | async-start | bytes 2162688 | tf_op jit(solution)/shard_map/reduce_scatter | solution.py:328
  1201.9 793.6 %reduce-scatter.23.cloned.1.call-start = ((), (), s32[]{:S(2)}) async-start(), calls=%async_computation.22 | async-start | bytes 2162688 | tf_op jit(solution)/shard_map/reduce_scatter | solution.py:329
  (112 other events, 3248.5 us)
Sparse Core Ops, SparseCore 0:
  11.1 59.5 all-gather.10
  73.8 55.5 all-gather.8
  132.5 57.0 all-gather.12
  192.6 55.6 all-gather.14
  251.2 107.1 all-gather.20
  361.3 86.7 all-gather.16
  451.0 52.3 all-gather.18
  506.2 52.7 all-gather.22
  893.8 149.0 reduce-scatter.18
  1045.6 137.7 reduce-scatter.24
  1186.1 131.9 reduce-scatter.12
  1320.8 131.6 reduce-scatter.10
  1455.3 131.6 reduce-scatter.14
  1589.6 131.6 reduce-scatter.16
  1724.0 133.9 reduce-scatter.20
  1860.7 134.7 reduce-scatter.22
